TPU v7x, 32 devices: a whole 2x2x4 slice. The times are simulated.
32 devices in a mesh: grp: 2 (over x), seq: 8 (over z, y), ten: 2 (over core).
Axes of the slice: x: 2, y: 2, z: 4, core: 2. Of those that a mesh axis runs over, the one named last changes fastest.
Arguments:
- queries: bfloat16 [1024, 4096], P(('grp', 'seq'), 'ten'), parts along dimension 0, may hold values from -128 to 128
- keys: bfloat16 [1024, 512], P(('grp', 'seq'), 'ten'), parts along dimension 0, may hold values from -6 to 6
- values: bfloat16 [1024, 512], P(('grp', 'seq'), 'ten'), parts along dimension 0, may hold values from -6 to 6
- hidden: bfloat16 [1024, 8192], P(('grp', 'seq')), parts along dimension 0, may hold values from -6 to 6
- norm_gain: float32 [8192], replicated, may hold values from 0.1 to 1.9
- retained_lists: int32 [1024], P(('grp', 'seq')), parts along dimension 0, may hold values from -1 to 63, as said below
- counts: int32 [16], P('grp'), parts along dimension 0, may hold values from 0 to 64, as said below
- affine_matrix: bfloat16 [8192, 5120], P('seq', 'ten'), may hold values from -0.0625 to 0.0625
- affine_offset_vector: float32 [5120], P('ten'), may hold values from -3 to 3
Outputs:
- context: float32 [1024, 4096], P(('grp', 'seq'), 'ten'), parts along dimension 0
- col_scores: float32 [1024], P(('grp', 'seq')), parts along dimension 0
- tier_third_mapped_triples: float32 [512, 5120], P(('grp', 'seq'), 'ten'), parts along dimension 0
There are 2 independent parts, one for each index of `grp`. A program takes and returns all parts, laid end to end along the dimension named above; an argument that names none is the same for every part. Nothing has to cross between parts.
Inputs may be any that keep to these rules, and one draw needn't show every extreme that they name: `retained_lists`: entries s*64 to (s+1)*64 - 1 hold, in their first counts[s] places, the kept local rows of shard s in rising order, and -1 after them. counts sum to 256; some shard keeps all its 64 rows.
All inputs are finite; a program needn't handle non-finite values.
Results may differ from a plain program's by a relative error of at most 0.0027.
Values may be sent and summed in bfloat16 or wider, within the bound.
A program may use at most 64 MiB of HBM per device.

v0:
```python
import math
import jax
import jax.numpy as jnp
from jax import lax
from jax.sharding import PartitionSpec as P

HEAD_SIZE = 128
QUERY_HEADS = 32


def block_length(key_count):
    return math.gcd(key_count, 512)


def heads_first(queries, kv_heads):
    partition_inner_lines = queries.shape[0]
    group_width = queries.shape[1] // (HEAD_SIZE * kv_heads)
    return (
        queries.reshape(partition_inner_lines, kv_heads, group_width, HEAD_SIZE)
        .transpose(1, 2, 0, 3)
        .reshape(kv_heads, group_width * partition_inner_lines, HEAD_SIZE)
    )


def masked_scores(query_heads, query_pos, key_block, offset):
    key_count = key_block.shape[0]
    kv_heads = query_heads.shape[0]
    key_head_rows = key_block.reshape(key_count, kv_heads, HEAD_SIZE)
    scores = jnp.einsum(
        "hrd,nhd->hrn", query_heads, key_head_rows, preferred_element_type=jnp.float32
    ) * HEAD_SIZE ** (-0.5)
    key_pos = offset + jnp.arange(key_count, dtype=jnp.int32)
    allowed = key_pos[None, None, :] <= query_pos[None, :, None]
    return (scores, allowed)


def attend(carried, pieces, query_heads, query_pos):
    key_piece, value_piece = pieces
    key_count = key_piece.shape[0]
    block_rows = block_length(key_count)
    block_total = key_count // block_rows
    kv_heads = query_heads.shape[0]
    key_blocks = key_piece.reshape(block_total, block_rows, key_piece.shape[1])
    value_blocks = value_piece.reshape(block_total, block_rows, value_piece.shape[1])

    def attend_step_block(state, inputs):
        row_max, row_sum, accumulated = state
        key_block, value_block, token_count = inputs
        scores, allowed = masked_scores(query_heads, query_pos, key_block, token_count * block_rows)
        new_max = jnp.maximum(row_max, jnp.max(jnp.where(allowed, scores, -1e30), axis=2))
        weights = jnp.where(allowed, jnp.exp(scores - new_max[:, :, None]), 0.0)
        factor = jnp.exp(row_max - new_max)
        row_sum = row_sum * factor + jnp.sum(weights, axis=2)
        value_head_rows = value_block.reshape(block_rows, kv_heads, HEAD_SIZE)
        update = jnp.einsum(
            "hrn,nhd->hrd",
            weights.astype(jnp.bfloat16),
            value_head_rows,
            preferred_element_type=jnp.float32,
        )
        accumulated = accumulated * factor[:, :, None] + update
        return ((new_max, row_sum, accumulated), None)

    state, unused = lax.scan(
        attend_step_block,
        carried,
        (key_blocks, value_blocks, jnp.arange(block_total, dtype=jnp.int32)),
    )
    return state


def column_terms(key_piece, query_heads, query_pos, log_total):
    key_count = key_piece.shape[0]
    block_rows = block_length(key_count)
    block_total = key_count // block_rows
    key_blocks = key_piece.reshape(block_total, block_rows, key_piece.shape[1])

    def column_step_block(state, inputs):
        key_block, token_count = inputs
        scores, allowed = masked_scores(query_heads, query_pos, key_block, token_count * block_rows)
        weights = jnp.where(allowed, jnp.exp(scores - log_total[:, :, None]), 0.0)
        return (state, jnp.sum(weights, axis=(0, 1)))

    unused, sums = lax.scan(
        column_step_block, jnp.float32(0.0), (key_blocks, jnp.arange(block_total, dtype=jnp.int32))
    )
    return sums.reshape(key_count)


def shards(
    queries,
    keys,
    values,
    hidden,
    norm_gain,
    retained_lists,
    counts,
    affine_matrix,
    affine_offset_vector,
):
    partition_inner_lines = queries.shape[0]
    kv_heads = keys.shape[1] // HEAD_SIZE
    group_width = queries.shape[1] // keys.shape[1]
    seq_index = lax.axis_index("seq")
    query_heads = heads_first(queries, kv_heads)
    query_pos = seq_index * partition_inner_lines + jnp.tile(
        jnp.arange(partition_inner_lines, dtype=jnp.int32), group_width
    )
    packed_rows = group_width * partition_inner_lines
    initial = (
        jnp.full((kv_heads, packed_rows), -1e30, jnp.float32),
        jnp.zeros((kv_heads, packed_rows), jnp.float32),
        jnp.zeros((kv_heads, packed_rows, HEAD_SIZE), jnp.float32),
    )
    row_max, row_sum, accumulated = attend(
        initial,
        (
            lax.all_gather(keys, "seq", axis=0, tiled=True),
            lax.all_gather(values, "seq", axis=0, tiled=True),
        ),
        query_heads,
        query_pos,
    )
    log_total = row_max + jnp.log(row_sum)
    column_part = column_terms(
        lax.all_gather(keys, "seq", axis=0, tiled=True), query_heads, query_pos, log_total
    )
    context = (
        (accumulated / row_sum[:, :, None])
        .reshape(kv_heads, group_width, partition_inner_lines, HEAD_SIZE)
        .transpose(2, 0, 1, 3)
        .reshape(partition_inner_lines, queries.shape[1])
    )
    column_rows = lax.psum_scatter(column_part, "seq", scatter_dimension=0, tiled=True)
    col_scores = lax.psum(column_rows, "ten") / QUERY_HEADS
    hidden_f = hidden.astype(jnp.float32)
    rescaled_activations = (
        hidden_f
        * lax.rsqrt(jnp.mean(hidden_f * hidden_f, axis=1, keepdims=True) + 1e-06)
        * norm_gain
    ).astype(jnp.bfloat16)
    selector = (
        retained_lists[:, None] == jnp.arange(partition_inner_lines, dtype=jnp.int32)[None, :]
    ).astype(jnp.bfloat16)
    chosen = jnp.dot(selector, rescaled_activations, preferred_element_type=jnp.float32).astype(
        jnp.bfloat16
    )
    sequence_total = lax.axis_size("seq")
    retained_total = sequence_total * partition_inner_lines // 2
    retained_element = jnp.arange(retained_total, dtype=jnp.int32)
    partition_finish_marks = jnp.cumsum(counts)
    holder_partition = jnp.sum(
        (partition_finish_marks[None, :] <= retained_element[:, None]).astype(jnp.int32), axis=1
    )
    starts = partition_finish_marks - counts
    opening_marks = jnp.sum(
        jnp.where(
            jnp.arange(sequence_total, dtype=jnp.int32)[None, :] == holder_partition[:, None],
            starts[None, :],
            0,
        ),
        axis=1,
    )
    retained_place_number = retained_element - opening_marks
    received = lax.all_to_all(chosen, "seq", split_axis=1, concat_axis=0, tiled=True)
    provenance = holder_partition * partition_inner_lines + retained_place_number
    compact = jnp.take(received, provenance, axis=0)
    projected = lax.psum_scatter(
        jnp.dot(compact, affine_matrix, preferred_element_type=jnp.float32),
        "seq",
        scatter_dimension=0,
        tiled=True,
    )
    tier_third_mapped_triples = projected + affine_offset_vector
    return (context, col_scores, tier_third_mapped_triples)


def solution(mesh):
    in_specs = (
        P(("grp", "seq"), "ten"),
        P(("grp", "seq"), "ten"),
        P(("grp", "seq"), "ten"),
        P(("grp", "seq"), None),
        P(),
        P(("grp", "seq")),
        P("grp"),
        P("seq", "ten"),
        P("ten"),
    )
    out_specs = (P(("grp", "seq"), "ten"), P(("grp", "seq")), P(("grp", "seq"), "ten"))
    return jax.shard_map(shards, mesh=mesh, in_specs=in_specs, out_specs=out_specs, check_vma=False)
```

profile of v0, /device:TPU:0, one launch (start us, length us, event | category | flops | bytes accessed | tf_op | source)
XLA Modules:
  0.0 152.0 jit_solution(15588536419003187684)
XLA Ops:
  7.2 1.5 %fusion = f32[64]{0:T(128)S(1)} fusion(bf16[64,8192]{1,0:T(8,128)(2,1)} %param.12), kind=kLoop, calls=%fused_computation.4 | loop fusion | flops 1572800 | bytes 1048832 | tf_op jit(solution)/shard_map/reduce_sum | solution.py:139
  8.7 1.7 %convolution_convert_fusion = bf16[64,8192]{1,0:T(8,128)(2,1)S(1)} fusion(bf16[64,8192]{1,0:T(8,128)(2,1)} %param.12, f32[8192]{0:T(1024)} %param.13, f32[64]{0:T(128)S(1)} %add_rsqrt_fusion, s32[64]{0:T(128)} %param.14), kind=kOutput, calls=%fused_computation.1 | convolution fusion | flops 69734400 | bytes 2130432 | tf_op jit(solution)/shard_map/dot_general | solution.py:145
  10.5 0.0 copy-start.4
  10.5 1.1 copy.48
  11.6 7.3 %all-to-all-start = ((bf16[64,8,1024]{2,0,1:T(8,128)(2,1)}), bf16[64,8,1024]{2,0,1:T(8,128)(2,1)S(1)}, u32[]{:S(2)}, u32[]{:S(2)}) async-start(bf16[64,8,1024]{2,0,1:T(8,128)(2,1)} %bitcast.32), calls=%async_computation | async-start | bytes 2097152 | tf_op jit(solution)/shard_map/all_to_all | solution.py:165
  18.9 0.0 reduce-scatter.2.cloned.1.call-start
  18.9 0.0 copy-done.4
  18.9 0.2 reduce-window.8
  19.1 0.1 convert_reduce_fusion
  19.2 0.1 select_reduce_fusion.2
  19.3 25.3 %all-to-all-done = bf16[64,8,1024]{2,0,1:T(8,128)(2,1)S(1)} async-done(((bf16[64,8,1024]{2,0,1:T(8,128)(2,1)}), bf16[64,8,1024]{2,0,1:T(8,128)(2,1)S(1)}, u32[]{:S(2)}, u32[]{:S(2)}) %all-to-all-start) | async-done | bytes 1048608 | tf_op jit(solution)/shard_map/all_to_all | solution.py:165
  44.6 1.2 gather_fusion
  45.8 5.6 %fusion.14 = f32[256,2560]{1,0:T(8,128)} fusion(bf16[1024,2560]{1,0:T(8,128)(2,1)} %param.16, bf16[256,1024]{1,0:T(8,128)(2,1)S(1)} %gather_fusion, pred[256]{0:T(512)(128)(4,1)S(1)} %compare_and_fusion), kind=kOutput, calls=%fused_computation.23 | convolution fusion | flops 1342439424 | bytes 8388864 | tf_op jit(solution)/shard_map/dot_general | solution.py:169
  51.4 0.0 copy-start
  51.4 0.0 copy-start.1
  51.4 0.0 copy-start.2
  51.4 0.0 reduce-scatter.2.cloned.1.call-update
  51.4 0.1 add.110
  51.5 0.8 copy-done
  52.4 0.1 copy.32
  52.4 0.0 copy-done.1
  52.4 31.7 %all_gather.7 = bf16[512,256]{1,0:T(8,128)(2,1)S(1)} all-gather(bf16[64,256]{1,0:T(8,128)(2,1)S(1)} %copy-done.1), channel_id=1, replica_groups=mesh['grp'=2,'seq'=8,'ten'=2] {'seq'}, dimensions={0}, use_global_device_ids=true | all-gather | bytes 294912 | tf_op jit(solution)/shard_map/all_gather | solution.py:118
  84.2 0.1 copy.33
  84.3 0.0 copy-done.2
  84.3 31.4 %all_gather.8 = bf16[512,256]{1,0:T(8,128)(2,1)S(1)} all-gather(bf16[64,256]{1,0:T(8,128)(2,1)S(1)} %copy-done.2), channel_id=1, replica_groups=mesh['grp'=2,'seq'=8,'ten'=2] {'seq'}, dimensions={0}, use_global_device_ids=true | all-gather | bytes 294912 | tf_op jit(solution)/shard_map/all_gather | solution.py:119
  115.7 0.1 copy.35
  115.9 0.2 iota_compare_fusion
  116.0 0.6 select_reduce_fusion.1
  116.7 0.5 fusion.3
  117.2 0.9 fusion.5
  118.2 0.0 copy-start.5
  118.2 0.0 copy-start.3
  118.2 0.3 copy.38
  118.5 1.0 copy.49
  119.5 0.0 copy-done.5
  119.5 0.6 dynamic-slice.2
  120.7 0.6 select_reduce_fusion
  121.3 19.1 %all-reduce = f32[512]{0:T(512)S(1)} all-reduce(f32[512]{0:T(512)S(1)} %select_reduce_fusion), channel_id=2, replica_groups=mesh['grp'=2,'seq'=8,'ten'=2] {'seq'}, use_global_device_ids=true, to_apply=%region_3.4.clone | all-reduce | flops 512 | bytes 4096
  140.4 0.1 dynamic-slice.3
  140.4 2.4 %psum.7 = f32[64]{0:T(128)S(1)} all-reduce(f32[64]{0:T(128)S(1)} %dynamic-slice.3), channel_id=1, replica_groups=mesh['grp'=2,'seq'=8,'ten'=2] {'ten'}, use_global_device_ids=true, to_apply=%region_4.5 | all-reduce | flops 64 | bytes 512 | tf_op jit(solution)/shard_map/psum | solution.py:135
  142.9 0.5 broadcast_multiply_fusion.1
  143.4 0.0 reduce-scatter.2.cloned.1.call-done
  143.4 0.0 copy-done.3
  143.4 1.7 %broadcast_add_fusion = f32[32,2560]{1,0:T(8,128)} fusion(f32[32,2560]{1,0:T(8,128)} %reduce-scatter.2.cloned.1.call-done, f32[2560]{0:T(1024)S(1)} %copy-done.3), kind=kLoop, calls=%fused_computation.27 | loop fusion | flops 81920 | bytes 665600 | tf_op jit(solution)/shard_map/add | solution.py:174
  (10 shorter events, 0.1 us)
Async XLA Ops:
  10.5 8.5 %copy-start.4 = (s32[8]{0:T(128)S(1)}, s32[8]{0:T(128)}, u32[]{:S(2)}) copy-start(s32[8]{0:T(128)} %param.15) | copy-start | bytes 100
  11.6 33.1 %all-to-all-start = ((bf16[64,8,1024]{2,0,1:T(8,128)(2,1)}), bf16[64,8,1024]{2,0,1:T(8,128)(2,1)S(1)}, u32[]{:S(2)}, u32[]{:S(2)}) async-start(bf16[64,8,1024]{2,0,1:T(8,128)(2,1)} %bitcast.32), calls=%async_computation | async-start | bytes 2097152 | tf_op jit(solution)/shard_map/all_to_all | solution.py:165
  18.9 124.5 %reduce-scatter.2.cloned.1.call-start = ((), (), s32[]{:S(2)}) async-start(), calls=%async_computation.2 | async-start | bytes 2949120 | tf_op jit(solution)/shard_map/reduce_scatter | solution.py:168
  51.4 0.9 copy-start
  51.4 1.1 copy-start.1
  51.4 32.9 %copy-start.2 = (bf16[64,256]{1,0:T(8,128)(2,1)S(1)}, bf16[64,256]{1,0:T(8,128)(2,1)}, u32[]{:S(2)}) copy-start(bf16[64,256]{1,0:T(8,128)(2,1)} %param.11) | copy-start | bytes 98308
  118.2 1.3 copy-start.5
  118.2 25.2 %copy-start.3 = (f32[2560]{0:T(1024)S(1)}, f32[2560]{0:T(1024)}, u32[]{:S(2)}) copy-start(f32[2560]{0:T(1024)} %param.17) | copy-start | bytes 30724
Sparse Core Ops, SparseCore 0:
  51.5 72.2 reduce-scatter.1
where the time goes:
time: 152 us
  blocking collectives  84.7 us (56%)
  waiting for transfers between devices  25.3 us (17%)
  between operations  14.8 us (10%)
  matrix products  8.9 us (6%)
  starting transfers between devices  7.35 us (5%)
  local copies, waits for them, and re-layouts  5.49 us (4%)
  other arithmetic  5.4 us (4%)
    all_gather x1, blocking collectives, shards(): lax.all_gather(keys, 'seq', axis=0, tiled=True)  31.7 us
    all_gather x1, blocking collectives, shards(): lax.all_gather(values, 'seq', axis=0, tiled=True)  31.4 us
    all_to_all x1, waiting for transfers between devices, shards(): lax.all_to_all(chosen, 'seq', split_axis=1, concat_axis=0, tiled=True)  25.3 us
    unnamed x1, blocking collectives  19.1 us
    all_to_all x1, starting transfers between devices, shards(): lax.all_to_all(chosen, 'seq', split_axis=1, concat_axis=0, tiled=True)  7.31 us
    dot_general x1, matrix products, shards(): jnp.dot(compact, affine_matrix, preferred_element_type=jnp.float32)  5.57 us
  transfers between devices with their start and end apart: 2, of which 1 were waited for; matrix products, arithmetic and copies ran while one was open for 4% of the time, Pallas kernels for 0%

commit v1 on v0

--- a/solution.py
+++ b/solution.py
@@ -162,7 +162,10 @@
         axis=1,
     )
     retained_place_number = retained_element - opening_marks
-    received = lax.all_to_all(chosen, "seq", split_axis=1, concat_axis=0, tiled=True)
+    received = jnp.concatenate(
+        lax.all_to_all(jnp.stack(jnp.split(chosen, lax.axis_size("seq"), axis=1)), "seq", 0, 0),
+        axis=0,
+    )
     provenance = holder_partition * partition_inner_lines + retained_place_number
     compact = jnp.take(received, provenance, axis=0)
     projected = lax.psum_scatter(

time: 152 us -> 156 us (1.026)
  local copies, waits for them, and re-layouts: 5.49 us -> 9.57 us
    unnamed x16 -> x23, local copies, waits for them, and re-layouts: 2.5 us -> 6.99 us
where the time goes in v1:
time: 156 us
  blocking collectives  84.6 us (54%)
  waiting for transfers between devices  25.3 us (16%)
  between operations  14.9 us (10%)
  local copies, waits for them, and re-layouts  9.57 us (6%)
  matrix products  8.91 us (6%)
  starting transfers between devices  7.35 us (5%)
  other arithmetic  5.4 us (3%)
    all_gather x1, blocking collectives, shards(): lax.all_gather(values, 'seq', axis=0, tiled=True)  31.9 us
    all_gather x1, blocking collectives, shards(): lax.all_gather(keys, 'seq', axis=0, tiled=True)  31.5 us
    all_to_all x1, waiting for transfers between devices, shards(): lax.all_to_all(jnp.stack(jnp.split(chosen, lax.axis_size('seq'), axis=1))...  25.3 us
    unnamed x1, blocking collectives  18.8 us
    all_to_all x1, starting transfers between devices, shards(): lax.all_to_all(jnp.stack(jnp.split(chosen, lax.axis_size('seq'), axis=1))...  7.31 us
    unnamed x23, local copies, waits for them, and re-layouts  6.99 us
    dot_general x1, matrix products, shards(): jnp.dot(compact, affine_matrix, preferred_element_type=jnp.float32)  5.56 us
  transfers between devices with their start and end apart: 2, of which 1 were waited for; matrix products, arithmetic and copies ran while one was open for 4% of the time, Pallas kernels for 0%

profile of v1, /device:TPU:0, one launch (start us, length us, event | category | flops | bytes accessed | tf_op | source)
XLA Modules:
  0.0 156.0 jit_solution(15554792290841420468)
XLA Ops:
  7.2 1.5 fusion
  8.7 1.7 %convolution_convert_fusion = bf16[64,8192]{1,0:T(8,128)(2,1)S(1)} fusion(bf16[64,8192]{1,0:T(8,128)(2,1)} %param.12, f32[8192]{0:T(1024)} %param.13, f32[64]{0:T(128)S(1)} %add_rsqrt_fusion, s32[64]{0:T(128)} %param.14), kind=kOutput, calls=%fused_computation.1 | convolution fusion | flops 69734400 | bytes 2130432 | tf_op jit(solution)/shard_map/dot_general | solution.py:145
  10.5 0.0 copy-start.4
  10.5 0.6 fusion.25
  11.1 0.7 fusion.24
  11.8 0.7 fusion.23
  12.5 0.7 fusion.22
  13.1 0.7 fusion.21
  13.8 0.6 fusion.20
  14.4 0.7 fusion.19
  15.1 0.7 fusion.18
  15.7 7.3 %all-to-all-start = ((bf16[8,64,1024]{2,1,0:T(8,128)(2,1)}), bf16[8,64,1024]{2,1,0:T(8,128)(2,1)S(1)}, u32[]{:S(2)}, u32[]{:S(2)}) async-start(bf16[8,64,1024]{2,1,0:T(8,128)(2,1)} %fusion.18), calls=%async_computation | async-start | bytes 2097152 | tf_op jit(solution)/shard_map/all_to_all | solution.py:166
  23.1 0.0 reduce-scatter.2.cloned.1.call-start
  23.1 0.0 copy-done.4
  23.1 0.2 reduce-window.8
  23.3 0.1 convert_reduce_fusion
  23.4 0.1 select_reduce_fusion.2
  23.5 25.3 %all-to-all-done = bf16[8,64,1024]{2,1,0:T(8,128)(2,1)S(1)} async-done(((bf16[8,64,1024]{2,1,0:T(8,128)(2,1)}), bf16[8,64,1024]{2,1,0:T(8,128)(2,1)S(1)}, u32[]{:S(2)}, u32[]{:S(2)}) %all-to-all-start) | async-done | bytes 1048608 | tf_op jit(solution)/shard_map/all_to_all | solution.py:166
  48.8 1.2 gather_fusion
  50.0 5.6 %fusion.14 = f32[256,2560]{1,0:T(8,128)} fusion(bf16[1024,2560]{1,0:T(8,128)(2,1)} %param.16, bf16[256,1024]{1,0:T(8,128)(2,1)S(1)} %gather_fusion, pred[256]{0:T(512)(128)(4,1)S(1)} %compare_and_fusion), kind=kOutput, calls=%fused_computation.22 | convolution fusion | flops 1342439424 | bytes 8388864 | tf_op jit(solution)/shard_map/dot_general | solution.py:172
  55.6 0.0 copy-start.1
  55.6 0.0 copy-start
  55.6 0.0 copy-start.2
  55.6 0.0 reduce-scatter.2.cloned.1.call-update
  55.6 0.7 copy-done.1
  56.3 31.9 %all_gather.8 = bf16[512,256]{1,0:T(8,128)(2,1)S(1)} all-gather(bf16[64,256]{1,0:T(8,128)(2,1)S(1)} %copy-done.1), channel_id=1, replica_groups=mesh['grp'=2,'seq'=8,'ten'=2] {'seq'}, dimensions={0}, use_global_device_ids=true | all-gather | bytes 294912 | tf_op jit(solution)/shard_map/all_gather | solution.py:119
  88.2 0.1 copy.32
  88.4 0.1 add.110
  88.4 0.0 copy-done
  88.5 0.1 copy.29
  88.6 0.0 copy-done.2
  88.6 31.5 %all_gather.7 = bf16[512,256]{1,0:T(8,128)(2,1)S(1)} all-gather(bf16[64,256]{1,0:T(8,128)(2,1)S(1)} %copy-done.2), channel_id=1, replica_groups=mesh['grp'=2,'seq'=8,'ten'=2] {'seq'}, dimensions={0}, use_global_device_ids=true | all-gather | bytes 294912 | tf_op jit(solution)/shard_map/all_gather | solution.py:118
  120.1 0.1 copy.30
  120.2 0.2 iota_compare_fusion
  120.4 0.6 select_reduce_fusion.1
  121.1 0.5 fusion.3
  121.6 1.0 fusion.5
  122.5 0.0 copy-start.5
  122.6 0.0 copy-start.3
  122.6 0.3 copy.35
  122.9 1.0 copy.42
  123.8 0.0 copy-done.5
  123.8 0.6 dynamic-slice.2
  125.1 0.6 select_reduce_fusion
  125.6 18.8 %all-reduce = f32[512]{0:T(512)S(1)} all-reduce(f32[512]{0:T(512)S(1)} %select_reduce_fusion), channel_id=2, replica_groups=mesh['grp'=2,'seq'=8,'ten'=2] {'seq'}, use_global_device_ids=true, to_apply=%region_3.4.clone | all-reduce | flops 512 | bytes 4096
  144.4 0.1 dynamic-slice.3
  144.5 2.4 %psum.7 = f32[64]{0:T(128)S(1)} all-reduce(f32[64]{0:T(128)S(1)} %dynamic-slice.3), channel_id=1, replica_groups=mesh['grp'=2,'seq'=8,'ten'=2] {'ten'}, use_global_device_ids=true, to_apply=%region_4.5 | all-reduce | flops 64 | bytes 512 | tf_op jit(solution)/shard_map/psum | solution.py:135
  147.0 0.5 broadcast_multiply_fusion.1
  147.5 0.0 reduce-scatter.2.cloned.1.call-done
  147.5 0.0 copy-done.3
  147.5 1.7 %broadcast_add_fusion = f32[32,2560]{1,0:T(8,128)} fusion(f32[32,2560]{1,0:T(8,128)} %reduce-scatter.2.cloned.1.call-done, f32[2560]{0:T(1024)S(1)} %copy-done.3), kind=kLoop, calls=%fused_computation.26 | loop fusion | flops 81920 | bytes 665600 | tf_op jit(solution)/shard_map/add | solution.py:177
  (10 shorter events, 0.1 us)
Async XLA Ops:
  10.5 12.6 %copy-start.4 = (s32[8]{0:T(128)S(1)}, s32[8]{0:T(128)}, u32[]{:S(2)}) copy-start(s32[8]{0:T(128)} %param.15) | copy-start | bytes 100
  15.7 33.1 %all-to-all-start = ((bf16[8,64,1024]{2,1,0:T(8,128)(2,1)}), bf16[8,64,1024]{2,1,0:T(8,128)(2,1)S(1)}, u32[]{:S(2)}, u32[]{:S(2)}) async-start(bf16[8,64,1024]{2,1,0:T(8,128)(2,1)} %fusion.18), calls=%async_computation | async-start | bytes 2097152 | tf_op jit(solution)/shard_map/all_to_all | solution.py:166
  23.1 124.4 %reduce-scatter.2.cloned.1.call-start = ((), (), s32[]{:S(2)}) async-start(), calls=%async_computation.2 | async-start | bytes 2949120 | tf_op jit(solution)/shard_map/reduce_scatter | solution.py:171
  55.6 0.8 copy-start.1
  55.6 32.9 %copy-start = (bf16[64,2048]{1,0:T(8,128)(2,1)S(1)}, bf16[64,2048]{1,0:T(8,128)(2,1)}, u32[]{:S(2)}) copy-start(bf16[64,2048]{1,0:T(8,128)(2,1)} %param.9) | copy-start | bytes 786436
  55.6 33.0 %copy-start.2 = (bf16[64,256]{1,0:T(8,128)(2,1)S(1)}, bf16[64,256]{1,0:T(8,128)(2,1)}, u32[]{:S(2)}) copy-start(bf16[64,256]{1,0:T(8,128)(2,1)} %param.10) | copy-start | bytes 98308
  122.5 1.3 copy-start.5
  122.6 24.9 %copy-start.3 = (f32[2560]{0:T(1024)S(1)}, f32[2560]{0:T(1024)}, u32[]{:S(2)}) copy-start(f32[2560]{0:T(1024)} %param.17) | copy-start | bytes 30724
Sparse Core Ops, SparseCore 0:
  55.7 71.7 reduce-scatter.1
